TPU v7x, 512 devices: a whole 4x4x16 slice. The times are simulated.
512 devices in a mesh: seq: 64 (over x, z), head: 8 (over y, core).
Axes of the slice: x: 4, y: 4, z: 16, core: 2. Of those that a mesh axis runs over, the one named last changes fastest.
Arguments:
- queries: bfloat16 [32768, 4096], P('seq', 'head'), may hold values from -6 to 6
- keys: bfloat16 [32768, 4096], P('seq', 'head'), may hold values from -0.5390625 to 0.5390625
- values: bfloat16 [32768, 4096], P('seq', 'head'), may hold values from -6 to 6
- log_decay: float32 [32, 32768], P('head', 'seq'), may hold values from -1 to 0, as said below
- out_weight: bfloat16 [4096, 3072], P('head'), may hold values from -0.125 to 0.125
Outputs:
- layer_out: bfloat16 [32768, 3072], P('seq', 'head')
Inputs may be any that keep to these rules, and one draw needn't show every extreme that they name: log_decay is negative.
All inputs are finite; a program needn't handle non-finite values.
Results may differ from a plain program's by a relative error of at most 0.018.
Values may be sent and summed in bfloat16 or wider, within the bound.
A program may use at most 64 MiB of HBM per device.

v0:
```python
import jax
import jax.numpy as jnp
from jax import lax
from jax.sharding import PartitionSpec as P


def prefix(x, axis, combine, identity):
    count, mine = (lax.axis_size(axis), lax.axis_index(axis))
    everything = jax.tree.map(
        lambda part, kind: lax.all_gather(part.astype(kind), axis), x, (jnp.bfloat16, jnp.bfloat16)
    )
    start = jax.tree.map(
        lambda part, zero: jnp.broadcast_to(jnp.asarray(zero, part.dtype), part.shape), x, identity
    )

    def turn(k, before):
        reached = k < mine
        new = combine(
            before, jax.tree.map(lambda part, own: part[k].astype(own.dtype), everything, x)
        )
        return jax.tree.map(lambda a, b: jnp.where(reached, a, b), new, before)

    return lax.fori_loop(0, count, turn, start)


def combine(earlier, later):
    return (earlier[0] * later[0], earlier[1] * later[0][:, None, None] + later[1])


def on_device(queries, keys, values, log_decay, out_weight):
    head_count, tok_rows = log_decay.shape
    head_size = queries.shape[1] // head_count
    query_heads = queries.reshape(tok_rows, head_count, head_size)
    key_heads = keys.reshape(tok_rows, head_count, head_size)
    value_heads = values.reshape(tok_rows, head_count, head_size)
    cumulative = jnp.cumsum(log_decay, axis=1)
    block_decay = cumulative[:, -1]
    scaled_keys = (
        key_heads.astype(jnp.float32) * jnp.exp(block_decay[:, None] - cumulative).T[:, :, None]
    ).astype(jnp.bfloat16)
    moments = jnp.einsum(
        "thd,the->hde", scaled_keys, value_heads, preferred_element_type=jnp.float32
    )
    identity = (
        jnp.ones((head_count,), jnp.float32),
        jnp.zeros((head_count, head_size, head_size), jnp.float32),
    )
    carried = prefix((jnp.exp(block_decay), moments), "seq", combine, identity)
    causal_mask = jnp.tril(jnp.ones((tok_rows, tok_rows), dtype=bool))
    scores = jnp.einsum("thd,shd->hts", query_heads, key_heads, preferred_element_type=jnp.float32)
    log_gaps = jnp.where(causal_mask[None], cumulative[:, :, None] - cumulative[:, None, :], 0.0)
    gaps = jnp.where(causal_mask[None], jnp.exp(log_gaps), 0.0)
    weighted = (scores * gaps).astype(jnp.bfloat16)
    intra_term = jnp.einsum(
        "hts,shd->thd", weighted, value_heads, preferred_element_type=jnp.float32
    )
    query_scaled = query_heads.astype(jnp.float32) * jnp.exp(cumulative).T[:, :, None]
    inter_term = jnp.einsum(
        "thd,hde->the", query_scaled, carried[1], precision=lax.Precision.HIGHEST
    )
    mixed_out = intra_term + inter_term
    normed = (
        mixed_out * lax.rsqrt(jnp.mean(mixed_out * mixed_out, axis=-1, keepdims=True) + 1e-05)
    ).astype(jnp.bfloat16)
    normed = normed.reshape(tok_rows, head_count * head_size)
    partial_out = jnp.dot(normed, out_weight, preferred_element_type=jnp.float32)
    summed = lax.psum_scatter(
        partial_out.astype(jnp.bfloat16), "head", scatter_dimension=1, tiled=True
    )
    return summed


def solution(mesh):
    return jax.shard_map(
        on_device,
        mesh=mesh,
        in_specs=(
            P("seq", "head"),
            P("seq", "head"),
            P("seq", "head"),
            P("head", "seq"),
            P("head", None),
        ),
        out_specs=P("seq", "head"),
        check_vma=False,
    )
```

profile of v0, /device:TPU:1, one launch (start us, length us, event | category | flops | bytes accessed | tf_op | source)
XLA Modules:
  0.0 299.2 jit_solution(176497033048423246)
XLA Ops:
  7.4 1.2 reduce-window.6
  9.3 2.1 copy.30
  11.3 2.1 convolution_convert_fusion.1
  13.6 1.3 dynamic-slice
  15.8 123.4 %all-reduce = bf16[256]{0:T(256)(128)(2,1)S(1)} all-reduce(bf16[256]{0:T(256)(128)(2,1)S(1)} %dynamic-update-slice), channel_id=2, replica_groups=mesh['seq'=64,'head'=8] {'seq'}, use_global_device_ids=true, to_apply=%add | all-reduce | flops 256 | bytes 1024
  140.1 4.6 %fusion.2 = f32[512,4,128]{0,2,1:T(8,128)} fusion(bf16[512,4,128]{0,2,1:T(8,128)(2,1)} %bitcast.76, f32[4,512]{1,0:T(4,128)S(1)} %bitcast.80, pred[512,512]{1,0:T(8,128)(4,1)} %iota_compare_fusion, bf16[512,512]{1,0:T(8,128)(2,1)} %param.9, bf16[512,512]{1,0:T(8,128)(2,1)} %param.7), kind=kOutput, calls=%fused_computation.6 | convolution fusion | flops 542113792 | bytes 2891776 | tf_op jit(solution)/shard_map/hts,shd->thd/dot_general | solution.py:54
  144.7 22.5 %all-gather.4.cloned.1.call-done = bf16[256,128,128]{2,1,0:T(8,128)(2,1)} async-done(((bf16[4,128,128]{2,1,0:T(8,128)(2,1)}), bf16[256,128,128]{2,1,0:T(8,128)(2,1)}) %all-gather.4.cloned.1.call-update) | async-done | bytes 8388624 | tf_op jit(solution)/shard_map/all_gather | solution.py:10
  167.2 67.4 %while.14 = (s32[]{:T(128)}, f32[4,128,128]{2,1,0:T(8,128)S(1)}, s32[]{:T(128)}, bf16[64,4]{1,0:T(8,128)(2,1)S(1)}, bf16[64,4,128,128]{3,2,1,0:T(8,128)(2,1)}, /*index=5*/s32[]{:T(128)}, s32[]{:T(128)}) while((s32[]{:T(128)}, f32[4,128,128]{2,1,0:T(8,128)S(1)}, s32[]{:T(128)}, bf16[64,4]{1,0:T(8,128)(2,1)S(1)}, ...), condition=%wide.region_3.4_spmd.clone, body=%wide.region_2.3_spmd.clone.sunk | while | flops 327688 | bytes 655505 | solution.py:23
  168.3 1.0 fusion.28
  169.3 1.0 fusion.28
  170.4 1.0 fusion.28
  171.4 1.0 fusion.28
  175.6 1.0 fusion.28
  179.9 1.0 fusion.28
  180.9 1.0 fusion.28
  185.1 1.0 fusion.28
  190.4 1.0 fusion.28
  195.7 1.0 fusion.28
  199.9 1.0 fusion.28
  200.9 1.0 fusion.28
  205.1 1.0 fusion.28
  210.4 1.0 fusion.28
  215.7 1.0 fusion.28
  219.9 1.0 fusion.28
  220.9 1.0 fusion.28
  225.2 1.0 fusion.28
  230.4 1.0 fusion.28
  234.6 2.8 multiply_reduce_fusion
  237.6 3.5 %convolution_convert_fusion = bf16[512,3072]{1,0:T(8,128)(2,1)} fusion(bf16[512,512]{0,1:T(8,128)(2,1)S(1)} %bitcast.74, bf16[512,3072]{1,0:T(8,128)(2,1)S(1)} %copy-done), kind=kOutput, calls=%fused_computation.3 | convolution fusion | flops 1612185600 | bytes 6815744 | tf_op jit(solution)/shard_map/dot_general | solution.py:66
  241.1 4.7 %copy.27 = bf16[512,3072]{0,1:T(8,128)(2,1)} copy(bf16[512,3072]{1,0:T(8,128)(2,1)} %convolution_convert_fusion) | data formatting | bytes 6291456
  245.8 44.7 %reduce-scatter.4.cloned.1.call-done = bf16[384,512]{1,0:T(8,128)(2,1)} async-done(((bf16[3072,512]{1,0:T(8,128)(2,1)}), bf16[384,512]{1,0:T(8,128)(2,1)}) %reduce-scatter.4.cloned.1.call-update) | async-done | bytes 393232
  290.5 1.9 copy.28
  (131 shorter events, 49.1 us)
Async XLA Ops:
  6.5 231.0 %copy-start = (bf16[512,3072]{1,0:T(8,128)(2,1)S(1)}, bf16[512,3072]{1,0:T(8,128)(2,1)}, u32[]{:S(2)}) copy-start(bf16[512,3072]{1,0:T(8,128)(2,1)} %param.11) | copy-start | bytes 9437188
  6.5 160.7 %all-gather.4.cloned.1.call-start = ((), (), s32[]{:S(2)}) async-start(), calls=%async_computation.1 | async-start | bytes 8519680 | tf_op jit(solution)/shard_map/all_gather | solution.py:10
  13.5 277.0 %reduce-scatter.4.cloned.1.call-start = ((), (), s32[]{:S(2)}) async-start(), calls=%async_computation.2 | async-start | bytes 3538944
Sparse Core Ops, SparseCore 0:
  13.6 153.5 all-gather.3
  245.9 44.5 reduce-scatter.3
where the time goes:
time: 302 us; the launch traced here: 299 us
  blocking collectives  123 us (41%)
  other arithmetic  67.9 us (22%)
  waiting for transfers between devices  67.2 us (22%)
  between operations  14.1 us (5%)
  matrix products  13.1 us (4%)
  local copies, waits for them, and re-layouts  11.5 us (4%)
    unnamed x1, blocking collectives  123 us
    select_n x64, other arithmetic, turn(): return jax.tree.map(lambda a, b: jnp.where(reached, a, b), new, before)  64.8 us
    unnamed x3, waiting for transfers between devices  44.7 us
    all_gather x1, waiting for transfers between devices, prefix(): lax.all_gather(part.astype(kind), axis)  22.5 us
    unnamed x9, local copies, waits for them, and re-layouts  8.19 us
  transfers between devices with their start and end apart: 2, of which 2 were waited for; matrix products, arithmetic and copies ran while one was open for 2% of the time, Pallas kernels for 0%

commit v1 on v0

v1 whole, which is shorter than its diff:
```python
import functools

import jax
import jax.numpy as jnp
from jax import lax
from jax.experimental import pallas as pl
from jax.experimental.pallas import tpu as pltpu
from jax.sharding import PartitionSpec as P

MESH = pl.DeviceIdType.MESH
F32, BF16 = jnp.float32, jnp.bfloat16


def far_first(n):
    return sorted(range(1, n), key=lambda k: (-min(k, n - k), k))


def kernel(
    xs, zs, ys,
    q_ref, k_ref, v_ref, g_ref, w_ref, out_ref,
    mom_out, mom_in, pref, pref_decay, tot_out, tot_in, car_out, car_in,
    intra, grown, normed, pair_out, pair_in, mine, ring_out, ring_in,
    s_mom, r_mom, s_tot, r_tot, s_car, r_car, s_pair, r_pair, s_ring, r_ring,
):
    seq, head = lax.axis_index("seq"), lax.axis_index("head")
    x, z = lax.div(seq, zs), lax.rem(seq, zs)
    y, c = lax.div(head, 2), lax.rem(head, 2)
    heads, toks = g_ref.shape
    dim = q_ref.shape[1] // heads
    rows = heads * dim // zs
    per = dim // rows
    cols = out_ref.shape[1]
    half = toks // 2

    def z_peer(k):
        return (x * zs + lax.rem(z + k, zs), head)

    def x_peer(k):
        return (lax.rem(x + k, xs) * zs + z, head)

    def y_peer(k):
        return (seq, lax.rem(y + k, ys) * 2 + c)

    partner = (seq, y * 2 + 1 - c)

    barrier = pltpu.get_barrier_semaphore()
    peers = [z_peer(k) for k in far_first(zs)] + [x_peer(k) for k in far_first(xs)]
    peers += [partner, y_peer(1), y_peer(ys - 1)]
    for peer in peers:
        pl.semaphore_signal(barrier, inc=1, device_id=peer, device_id_type=MESH)

    g = g_ref[...]
    low = lax.broadcasted_iota(jnp.int32, (toks, toks), 0) >= lax.broadcasted_iota(
        jnp.int32, (toks, toks), 1
    )
    tri = low.astype(F32)
    cum_row = lax.dot_general(
        g, tri, (((1,), (1,)), ((), ())), precision=lax.Precision.HIGHEST,
        preferred_element_type=F32,
    )
    cum_col = cum_row.T
    grown[...] = jnp.exp(cum_col)

    for h in range(heads):
        lanes = slice(h * dim, (h + 1) * dim)
        col = cum_col[:, h : h + 1]
        end = cum_col[toks - 1 : toks, h : h + 1]
        scaled = (k_ref[:, lanes].astype(F32) * jnp.exp(end - col)).astype(BF16)
        moments = lax.dot_general(
            scaled, v_ref[:, lanes], (((0,), (0,)), ((), ())), preferred_element_type=F32
        )
        decay = jnp.broadcast_to(jnp.exp(end), (8, dim))
        coarse = decay.astype(BF16).astype(F32)
        tile = jnp.concatenate([coarse, decay - coarse], axis=0).astype(BF16)
        for p in range(per):
            mom_out[h * per + p, 0:rows, :] = moments[p * rows : (p + 1) * rows].astype(BF16)
            mom_out[h * per + p, rows : rows + 16, :] = tile

    pl.semaphore_wait(barrier, len(peers))

    mom_copies = []
    for k in far_first(zs):
        mom_copies.append(
            pltpu.make_async_remote_copy(
                src_ref=mom_out.at[lax.rem(z + k, zs)], dst_ref=mom_in.at[z],
                send_sem=s_mom.at[k], recv_sem=r_mom.at[k],
                device_id=z_peer(k), device_id_type=MESH,
            )
        )
        mom_copies[-1].start()
    mom_in[z] = mom_out[z]

    def within(h):
        lanes = slice(h * dim, (h + 1) * dim)
        scores = lax.dot_general(
            q_ref[:, lanes], k_ref[:, lanes], (((1,), (1,)), ((), ())),
            preferred_element_type=F32,
        )
        gap = cum_col[:, h : h + 1] - cum_row[h : h + 1, :]
        weighted = (scores * jnp.exp(jnp.where(low, gap, -jnp.inf))).astype(BF16)
        intra[:, lanes] = jnp.dot(weighted, v_ref[:, lanes], preferred_element_type=F32)

    for h in range(heads // 2):
        within(h)

    for copy in mom_copies:
        copy.wait_recv()

    state = jnp.zeros((rows, dim), F32)
    decay = jnp.ones((8, dim), F32)
    for j in range(zs):
        pref[j] = state
        pref_decay[j] = decay
        step = mom_in[j, rows : rows + 16, :].astype(F32)
        step = step[0:8] + step[8:16]
        state = state * step[0:1] + mom_in[j, 0:rows, :].astype(F32)
        decay = decay * step
    tot_out[0:rows, :] = state
    tot_out[rows : rows + 8, :] = decay
    tot_copies = []
    for k in far_first(xs):
        tot_copies.append(
            pltpu.make_async_remote_copy(
                src_ref=tot_out, dst_ref=tot_in.at[x],
                send_sem=s_tot.at[k], recv_sem=r_tot.at[k],
                device_id=x_peer(k), device_id_type=MESH,
            )
        )
        tot_copies[-1].start()
    tot_in[x] = tot_out[...]
    for copy in tot_copies:
        copy.wait_recv()

    before = jnp.zeros((rows, dim), F32)
    for j in range(xs):
        new = before * tot_in[j, rows : rows + 1, :] + tot_in[j, 0:rows, :]
        before = jnp.where(j < x, new, before)
    for j in range(zs):
        car_out[j] = (pref[j] + pref_decay[j, 0:1, :] * before).astype(BF16)
    car_copies = []
    for k in far_first(zs):
        car_copies.append(
            pltpu.make_async_remote_copy(
                src_ref=car_out.at[lax.rem(z + k, zs)], dst_ref=car_in.at[z],
                send_sem=s_car.at[k], recv_sem=r_car.at[k],
                device_id=z_peer(k), device_id_type=MESH,
            )
        )
        car_copies[-1].start()
    car_in[z] = car_out[z]

    for h in range(heads // 2, heads):
        within(h)

    for copy in car_copies:
        copy.wait_recv()

    for h in range(heads):
        lanes = slice(h * dim, (h + 1) * dim)
        carried = car_in[h * per : (h + 1) * per].reshape(dim, dim)
        inter = jnp.dot(q_ref[:, lanes], carried, preferred_element_type=F32)
        mixed = intra[:, lanes] + inter * grown[:, h : h + 1]
        scale = lax.rsqrt(jnp.mean(mixed * mixed, axis=-1, keepdims=True) + 1e-05)
        normed[:, lanes] = (mixed * scale).astype(BF16)

    def project(to_y, to_c):
        start = pl.multiple_of((to_y * 2 + to_c) * cols, 128)
        return jnp.dot(
            normed[...], w_ref[:, pl.ds(start, cols)], preferred_element_type=F32
        ).astype(BF16)

    order = (2, 1, 3, 0)
    pair_copies = {}
    for o in order:
        pair_out[o] = project(lax.rem(y + o, ys), 1 - c)
        pair_copies[o] = pltpu.make_async_remote_copy(
            src_ref=pair_out.at[o], dst_ref=pair_in.at[o],
            send_sem=s_pair.at[o], recv_sem=r_pair.at[o],
            device_id=partner, device_id_type=MESH,
        )
        pair_copies[o].start()

    def ring(slot, source, k):
        copy = pltpu.make_async_remote_copy(
            src_ref=source, dst_ref=ring_in.at[slot],
            send_sem=s_ring.at[slot], recv_sem=r_ring.at[slot],
            device_id=y_peer(k), device_id_type=MESH,
        )
        copy.start()
        return copy

    top, bottom = slice(0, half), slice(half, toks)
    copies = [None] * 6
    for o in order:
        own = project(lax.rem(y + o, ys), c).astype(F32)
        pair_copies[o].wait_recv()
        both = own + pair_in[o].astype(F32)
        mine[o] = both.astype(BF16)
        if o == 2:
            copies[0] = ring(0, mine.at[2, pl.ds(0, half)], 1)
            copies[1] = ring(1, mine.at[2, pl.ds(half, half)], ys - 1)
        elif o == 1:
            copies[2] = ring(2, mine.at[1, pl.ds(half, half)], 1)
        elif o == 3:
            copies[3] = ring(3, mine.at[3, pl.ds(0, half)], ys - 1)
    copies[0].wait_recv()
    ring_out[0] = (mine[1, top, :].astype(F32) + ring_in[0].astype(F32)).astype(BF16)
    copies[4] = ring(4, ring_out.at[0], 1)
    copies[1].wait_recv()
    ring_out[1] = (mine[3, bottom, :].astype(F32) + ring_in[1].astype(F32)).astype(BF16)
    copies[5] = ring(5, ring_out.at[1], ys - 1)
    copies[2].wait_recv()
    copies[3].wait_recv()
    copies[4].wait_recv()
    out_ref[top, :] = (
        mine[0, top, :].astype(F32) + ring_in[3].astype(F32) + ring_in[4].astype(F32)
    ).astype(BF16)
    copies[5].wait_recv()
    out_ref[bottom, :] = (
        mine[0, bottom, :].astype(F32) + ring_in[2].astype(F32) + ring_in[5].astype(F32)
    ).astype(BF16)

    for copy in mom_copies + tot_copies + car_copies + list(pair_copies.values()) + copies:
        copy.wait_send()


def on_device(xs, zs, ys, queries, keys, values, log_decay, out_weight):
    heads, toks = log_decay.shape
    feat = queries.shape[1]
    dim = feat // heads
    rows = feat // zs
    cols = out_weight.shape[1] // (ys * 2)
    vmem = pl.BlockSpec(memory_space=pltpu.VMEM)
    dma = pltpu.SemaphoreType.DMA
    return pl.pallas_call(
        functools.partial(kernel, xs, zs, ys),
        out_shape=jax.ShapeDtypeStruct((toks, cols), BF16),
        in_specs=[vmem] * 5,
        out_specs=vmem,
        scratch_shapes=[
            pltpu.VMEM((zs, rows + 16, dim), BF16),
            pltpu.VMEM((zs, rows + 16, dim), BF16),
            pltpu.VMEM((zs, rows, dim), F32),
            pltpu.VMEM((zs, 8, dim), F32),
            pltpu.VMEM((rows + 8, dim), F32),
            pltpu.VMEM((xs, rows + 8, dim), F32),
            pltpu.VMEM((zs, rows, dim), BF16),
            pltpu.VMEM((zs, rows, dim), BF16),
            pltpu.VMEM((toks, feat), F32),
            pltpu.VMEM((toks, heads), F32),
            pltpu.VMEM((toks, feat), BF16),
            pltpu.VMEM((ys, toks, cols), BF16),
            pltpu.VMEM((ys, toks, cols), BF16),
            pltpu.VMEM((ys, toks, cols), BF16),
            pltpu.VMEM((2, toks // 2, cols), BF16),
            pltpu.VMEM((6, toks // 2, cols), BF16),
            dma((zs,)), dma((zs,)), dma((xs,)), dma((xs,)), dma((zs,)), dma((zs,)),
            dma((ys,)), dma((ys,)), dma((6,)), dma((6,)),
        ],
        compiler_params=pltpu.CompilerParams(
            collective_id=0, has_side_effects=True, vmem_limit_bytes=60 * 1024 * 1024
        ),
    )(queries, keys, values, log_decay, out_weight)


def solution(mesh, xs=4):
    zs = mesh.shape["seq"] // xs
    ys = mesh.shape["head"] // 2
    return jax.shard_map(
        functools.partial(on_device, xs, zs, ys),
        mesh=mesh,
        in_specs=(
            P("seq", "head"),
            P("seq", "head"),
            P("seq", "head"),
            P("head", "seq"),
            P("head", None),
        ),
        out_specs=P("seq", "head"),
        check_vma=False,
    )
```

time: 302 us -> 64.5 us (0.21)
  blocking collectives: 123 us -> 0 us
  other arithmetic: 67.9 us -> 0 us
  waiting for transfers between devices: 67.2 us -> 0 us
  Pallas kernels: 0 us -> 62.5 us
  between operations: 14.1 us -> 0.01 us
  matrix products: 13.1 us -> 0 us
  local copies, waits for them, and re-layouts: 11.5 us -> 1.78 us
    unnamed x1 -> x0, blocking collectives: 123 us -> none
    select_n x64 -> x0, other arithmetic: 64.8 us -> none  [turn(): return jax.tree.map(lambda a, b: jnp.where(reached, a, b), new, before)]
    pallas_call x0 -> x1, Pallas kernels: none -> 62.5 us  [on_device(): pl.pallas_call(functools.partial(kernel, xs, zs, ys), out_shape=jax.Shape...]
    unnamed x3 -> x0, waiting for transfers between devices: 44.7 us -> none
    all_gather x1 -> x0, waiting for transfers between devices: 22.5 us -> none  [prefix(): lax.all_gather(part.astype(kind), axis)]
    dot_general x4 -> x0, matrix products: 13.1 us -> none  [the longest x1 4.56 us: on_device(): jnp.einsum('hts,shd->thd', weighted, value_heads, preferred_element_type=...]
    unnamed x9 -> x1, local copies, waits for them, and re-layouts: 8.19 us -> 1.78 us
  transfers between devices with their start and end apart: 2 -> 0, of which waited for: 2 -> 0; matrix products, arithmetic and copies ran while one was open for 2% -> 0% of each run, Pallas kernels for 0% -> 0%
where the time goes in v1:
time: 64.5 us; the launch traced here: 64.3 us
  Pallas kernels  62.5 us (97%)
  local copies, waits for them, and re-layouts  1.78 us (3%)
    pallas_call x1, Pallas kernels, on_device(): pl.pallas_call(functools.partial(kernel, xs, zs, ys), out_shape=jax.Shape...  62.5 us
    unnamed x1, local copies, waits for them, and re-layouts  1.78 us

profile of v1, /device:TPU:1, one launch (start us, length us, event | category | flops | bytes accessed | tf_op | source)
XLA Modules:
  0.0 64.3 jit_solution(4415854095631190014)
XLA Ops:
  0.0 62.5 %shard_map.55 = bf16[512,384]{1,0:T(8,128)(2,1)} custom-call(bf16[512,512]{1,0:T(8,128)(2,1)} %q_ref.1, bf16[512,512]{1,0:T(8,128)(2,1)} %k_ref.1, bf16[512,512]{1,0:T(8,128)(2,1)} %v_ref.1, f32[4,512]{1,0:T(4,128)} %g_ref.1, bf16[512,3072]{1,0:T(8,128)(2,1)} %w_ref.1), custom_call_target="tpu_custom_call" | custom-call | tf_op jit(solution)/shard_map/pallas_call | solution.py:235
  62.5 1.8 %copy.7 = bf16[512,384]{1,0:T(8,128)(2,1)} copy(bf16[512,384]{1,0:T(8,128)(2,1)} %shard_map.55) | data formatting | bytes 786432

commit v2 on v1

--- a/solution.py
+++ b/solution.py
@@ -17,10 +17,13 @@
 
 def kernel(
     xs, zs, ys,
-    q_ref, k_ref, v_ref, g_ref, w_ref, out_ref,
-    mom_out, mom_in, pref, pref_decay, tot_out, tot_in, car_out, car_in,
+    q_hbm, k_hbm, v_hbm, g_hbm, w_hbm, out_ref,
+    q_ref, k_ref, v_ref, g_ref, w_ref,
+    mom_out, mom_in, dec_out, dec_in, pref, pref_decay,
+    tot_out, tot_in, end_out, end_in, car_out, car_in,
     intra, grown, normed, pair_out, pair_in, mine, ring_out, ring_in,
-    s_mom, r_mom, s_tot, r_tot, s_car, r_car, s_pair, r_pair, s_ring, r_ring,
+    s_mom, r_mom, s_dec, r_dec, s_tot, r_tot, s_end, r_end, s_car, r_car,
+    s_pair, r_pair, s_ring, r_ring, s_load,
 ):
     seq, head = lax.axis_index("seq"), lax.axis_index("head")
     x, z = lax.div(seq, zs), lax.rem(seq, zs)
@@ -49,6 +52,14 @@
     for peer in peers:
         pl.semaphore_signal(barrier, inc=1, device_id=peer, device_id_type=MESH)
 
+    loads = []
+    for n, (source, target) in enumerate(
+        ((g_hbm, g_ref), (k_hbm, k_ref), (v_hbm, v_ref), (q_hbm, q_ref), (w_hbm, w_ref))
+    ):
+        loads.append(pltpu.make_async_copy(source, target, s_load.at[n]))
+        loads[-1].start()
+
+    loads[0].wait()
     g = g_ref[...]
     low = lax.broadcasted_iota(jnp.int32, (toks, toks), 0) >= lax.broadcasted_iota(
         jnp.int32, (toks, toks), 1
@@ -61,6 +72,8 @@
     cum_col = cum_row.T
     grown[...] = jnp.exp(cum_col)
 
+    loads[1].wait()
+    loads[2].wait()
     for h in range(heads):
         lanes = slice(h * dim, (h + 1) * dim)
         col = cum_col[:, h : h + 1]
@@ -69,12 +82,9 @@
         moments = lax.dot_general(
             scaled, v_ref[:, lanes], (((0,), (0,)), ((), ())), preferred_element_type=F32
         )
-        decay = jnp.broadcast_to(jnp.exp(end), (8, dim))
-        coarse = decay.astype(BF16).astype(F32)
-        tile = jnp.concatenate([coarse, decay - coarse], axis=0).astype(BF16)
+        dec_out[h] = jnp.broadcast_to(jnp.exp(end), (1, dim))
         for p in range(per):
-            mom_out[h * per + p, 0:rows, :] = moments[p * rows : (p + 1) * rows].astype(BF16)
-            mom_out[h * per + p, rows : rows + 16, :] = tile
+            mom_out[h * per + p] = moments[p * rows : (p + 1) * rows].astype(BF16)
 
     pl.semaphore_wait(barrier, len(peers))
 
@@ -88,7 +98,17 @@
             )
         )
         mom_copies[-1].start()
+        mom_copies.append(
+            pltpu.make_async_remote_copy(
+                src_ref=dec_out.at[lax.div(lax.rem(z + k, zs), per)], dst_ref=dec_in.at[z],
+                send_sem=s_dec.at[k], recv_sem=r_dec.at[k],
+                device_id=z_peer(k), device_id_type=MESH,
+            )
+        )
+        mom_copies[-1].start()
     mom_in[z] = mom_out[z]
+    dec_in[z] = dec_out[lax.div(z, per)]
+    loads[3].wait()
 
     def within(h):
         lanes = slice(h * dim, (h + 1) * dim)
@@ -107,16 +127,14 @@
         copy.wait_recv()
 
     state = jnp.zeros((rows, dim), F32)
-    decay = jnp.ones((8, dim), F32)
+    decay = jnp.ones((1, dim), F32)
     for j in range(zs):
         pref[j] = state
         pref_decay[j] = decay
-        step = mom_in[j, rows : rows + 16, :].astype(F32)
-        step = step[0:8] + step[8:16]
-        state = state * step[0:1] + mom_in[j, 0:rows, :].astype(F32)
-        decay = decay * step
-    tot_out[0:rows, :] = state
-    tot_out[rows : rows + 8, :] = decay
+        state = state * dec_in[j] + mom_in[j].astype(F32)
+        decay = decay * dec_in[j]
+    tot_out[...] = state.astype(BF16)
+    end_out[...] = decay
     tot_copies = []
     for k in far_first(xs):
         tot_copies.append(
@@ -127,16 +145,25 @@
             )
         )
         tot_copies[-1].start()
+        tot_copies.append(
+            pltpu.make_async_remote_copy(
+                src_ref=end_out, dst_ref=end_in.at[x],
+                send_sem=s_end.at[k], recv_sem=r_end.at[k],
+                device_id=x_peer(k), device_id_type=MESH,
+            )
+        )
+        tot_copies[-1].start()
     tot_in[x] = tot_out[...]
+    end_in[x] = end_out[...]
     for copy in tot_copies:
         copy.wait_recv()
 
     before = jnp.zeros((rows, dim), F32)
     for j in range(xs):
-        new = before * tot_in[j, rows : rows + 1, :] + tot_in[j, 0:rows, :]
+        new = before * end_in[j] + tot_in[j].astype(F32)
         before = jnp.where(j < x, new, before)
     for j in range(zs):
-        car_out[j] = (pref[j] + pref_decay[j, 0:1, :] * before).astype(BF16)
+        car_out[j] = (pref[j] + pref_decay[j] * before).astype(BF16)
     car_copies = []
     for k in far_first(zs):
         car_copies.append(
@@ -169,9 +196,10 @@
             normed[...], w_ref[:, pl.ds(start, cols)], preferred_element_type=F32
         ).astype(BF16)
 
-    order = (2, 1, 3, 0)
+    loads[4].wait()
     pair_copies = {}
-    for o in order:
+
+    def give(o):
         pair_out[o] = project(lax.rem(y + o, ys), 1 - c)
         pair_copies[o] = pltpu.make_async_remote_copy(
             src_ref=pair_out.at[o], dst_ref=pair_in.at[o],
@@ -180,6 +208,11 @@
         )
         pair_copies[o].start()
 
+    def keep(o):
+        own = project(lax.rem(y + o, ys), c).astype(F32)
+        pair_copies[o].wait_recv()
+        mine[o] = (own + pair_in[o].astype(F32)).astype(BF16)
+
     def ring(slot, source, k):
         copy = pltpu.make_async_remote_copy(
             src_ref=source, dst_ref=ring_in.at[slot],
@@ -191,18 +224,18 @@
 
     top, bottom = slice(0, half), slice(half, toks)
     copies = [None] * 6
-    for o in order:
-        own = project(lax.rem(y + o, ys), c).astype(F32)
-        pair_copies[o].wait_recv()
-        both = own + pair_in[o].astype(F32)
-        mine[o] = both.astype(BF16)
-        if o == 2:
-            copies[0] = ring(0, mine.at[2, pl.ds(0, half)], 1)
-            copies[1] = ring(1, mine.at[2, pl.ds(half, half)], ys - 1)
-        elif o == 1:
-            copies[2] = ring(2, mine.at[1, pl.ds(half, half)], 1)
-        elif o == 3:
-            copies[3] = ring(3, mine.at[3, pl.ds(0, half)], ys - 1)
+    give(2)
+    give(1)
+    keep(2)
+    copies[0] = ring(0, mine.at[2, pl.ds(0, half)], 1)
+    copies[1] = ring(1, mine.at[2, pl.ds(half, half)], ys - 1)
+    give(3)
+    keep(1)
+    copies[2] = ring(2, mine.at[1, pl.ds(half, half)], 1)
+    give(0)
+    keep(3)
+    copies[3] = ring(3, mine.at[3, pl.ds(0, half)], ys - 1)
+    keep(0)
     copies[0].wait_recv()
     ring_out[0] = (mine[1, top, :].astype(F32) + ring_in[0].astype(F32)).astype(BF16)
     copies[4] = ring(4, ring_out.at[0], 1)
@@ -235,15 +268,24 @@
     return pl.pallas_call(
         functools.partial(kernel, xs, zs, ys),
         out_shape=jax.ShapeDtypeStruct((toks, cols), BF16),
-        in_specs=[vmem] * 5,
+        in_specs=[pl.BlockSpec(memory_space=pl.ANY)] * 5,
         out_specs=vmem,
         scratch_shapes=[
-            pltpu.VMEM((zs, rows + 16, dim), BF16),
-            pltpu.VMEM((zs, rows + 16, dim), BF16),
+            pltpu.VMEM((toks, feat), BF16),
+            pltpu.VMEM((toks, feat), BF16),
+            pltpu.VMEM((toks, feat), BF16),
+            pltpu.VMEM((heads, toks), F32),
+            pltpu.VMEM(out_weight.shape, BF16),
+            pltpu.VMEM((zs, rows, dim), BF16),
+            pltpu.VMEM((zs, rows, dim), BF16),
+            pltpu.VMEM((heads, 1, dim), F32),
+            pltpu.VMEM((zs, 1, dim), F32),
             pltpu.VMEM((zs, rows, dim), F32),
-            pltpu.VMEM((zs, 8, dim), F32),
-            pltpu.VMEM((rows + 8, dim), F32),
-            pltpu.VMEM((xs, rows + 8, dim), F32),
+            pltpu.VMEM((zs, 1, dim), F32),
+            pltpu.VMEM((rows, dim), BF16),
+            pltpu.VMEM((xs, rows, dim), BF16),
+            pltpu.VMEM((1, dim), F32),
+            pltpu.VMEM((xs, 1, dim), F32),
             pltpu.VMEM((zs, rows, dim), BF16),
             pltpu.VMEM((zs, rows, dim), BF16),
             pltpu.VMEM((toks, feat), F32),
@@ -254,8 +296,9 @@
             pltpu.VMEM((ys, toks, cols), BF16),
             pltpu.VMEM((2, toks // 2, cols), BF16),
             pltpu.VMEM((6, toks // 2, cols), BF16),
-            dma((zs,)), dma((zs,)), dma((xs,)), dma((xs,)), dma((zs,)), dma((zs,)),
-            dma((ys,)), dma((ys,)), dma((6,)), dma((6,)),
+            dma((zs,)), dma((zs,)), dma((zs,)), dma((zs,)),
+            dma((xs,)), dma((xs,)), dma((xs,)), dma((xs,)), dma((zs,)), dma((zs,)),
+            dma((ys,)), dma((ys,)), dma((6,)), dma((6,)), dma((5,)),
         ],
         compiler_params=pltpu.CompilerParams(
             collective_id=0, has_side_effects=True, vmem_limit_bytes=60 * 1024 * 1024

time: 64.5 us -> 59.9 us (0.929)
  Pallas kernels: 62.5 us -> 58 us
    pallas_call x1, Pallas kernels: 62.5 us -> 58 us  [on_device(): pl.pallas_call(functools.partial(kernel, xs, zs, ys), out_shape=jax.Shape...]
where the time goes in v2:
time: 59.9 us; the launch traced here: 59.8 us
  Pallas kernels  58 us (97%)
  local copies, waits for them, and re-layouts  1.78 us (3%)
    pallas_call x1, Pallas kernels, on_device(): pl.pallas_call(functools.partial(kernel, xs, zs, ys), out_shape=jax.Shape...  58 us
    unnamed x1, local copies, waits for them, and re-layouts  1.78 us

profile of v2, /device:TPU:1, one launch (start us, length us, event | category | flops | bytes accessed | tf_op | source)
XLA Modules:
  0.0 59.8 jit_solution(11842868790366935391)
XLA Ops:
  0.0 58.0 %shard_map.55 = bf16[512,384]{1,0:T(8,128)(2,1)} custom-call(bf16[512,512]{1,0:T(8,128)(2,1)} %q_hbm.1, bf16[512,512]{1,0:T(8,128)(2,1)} %k_hbm.1, bf16[512,512]{1,0:T(8,128)(2,1)} %v_hbm.1, f32[4,512]{1,0:T(4,128)} %g_hbm.1, bf16[512,3072]{1,0:T(8,128)(2,1)} %w_hbm.1), custom_call_target="tpu_custom_call" | custom-call | tf_op jit(solution)/shard_map/pallas_call | solution.py:268
  58.0 1.8 %copy.7 = bf16[512,384]{1,0:T(8,128)(2,1)} copy(bf16[512,384]{1,0:T(8,128)(2,1)} %shard_map.55) | data formatting | bytes 786432

commit v3 on v2

--- a/solution.py
+++ b/solution.py
@@ -182,36 +182,39 @@
     for copy in car_copies:
         copy.wait_recv()
 
-    for h in range(heads):
-        lanes = slice(h * dim, (h + 1) * dim)
-        carried = car_in[h * per : (h + 1) * per].reshape(dim, dim)
-        inter = jnp.dot(q_ref[:, lanes], carried, preferred_element_type=F32)
-        mixed = intra[:, lanes] + inter * grown[:, h : h + 1]
-        scale = lax.rsqrt(jnp.mean(mixed * mixed, axis=-1, keepdims=True) + 1e-05)
-        normed[:, lanes] = (mixed * scale).astype(BF16)
-
-    def project(to_y, to_c):
+    top, bottom = slice(0, half), slice(half, toks)
+
+    def finish(part):
+        for h in range(heads):
+            lanes = slice(h * dim, (h + 1) * dim)
+            carried = car_in[h * per : (h + 1) * per].reshape(dim, dim)
+            inter = jnp.dot(q_ref[part, lanes], carried, preferred_element_type=F32)
+            mixed = intra[part, lanes] + inter * grown[part, h : h + 1]
+            scale = lax.rsqrt(jnp.mean(mixed * mixed, axis=-1, keepdims=True) + 1e-05)
+            normed[part, lanes] = (mixed * scale).astype(BF16)
+
+    def project(to_y, to_c, part):
         start = pl.multiple_of((to_y * 2 + to_c) * cols, 128)
         return jnp.dot(
-            normed[...], w_ref[:, pl.ds(start, cols)], preferred_element_type=F32
+            normed[part, :], w_ref[:, pl.ds(start, cols)], preferred_element_type=F32
         ).astype(BF16)
 
-    loads[4].wait()
     pair_copies = {}
 
-    def give(o):
-        pair_out[o] = project(lax.rem(y + o, ys), 1 - c)
-        pair_copies[o] = pltpu.make_async_remote_copy(
-            src_ref=pair_out.at[o], dst_ref=pair_in.at[o],
-            send_sem=s_pair.at[o], recv_sem=r_pair.at[o],
+    def give(o, part):
+        n, rows_of = part.start // half, pl.ds(part.start, half)
+        pair_out[o, part, :] = project(lax.rem(y + o, ys), 1 - c, part)
+        pair_copies[o, n] = pltpu.make_async_remote_copy(
+            src_ref=pair_out.at[o, rows_of], dst_ref=pair_in.at[o, rows_of],
+            send_sem=s_pair.at[2 * o + n], recv_sem=r_pair.at[2 * o + n],
             device_id=partner, device_id_type=MESH,
         )
-        pair_copies[o].start()
-
-    def keep(o):
-        own = project(lax.rem(y + o, ys), c).astype(F32)
-        pair_copies[o].wait_recv()
-        mine[o] = (own + pair_in[o].astype(F32)).astype(BF16)
+        pair_copies[o, n].start()
+
+    def keep(o, part):
+        own = project(lax.rem(y + o, ys), c, part).astype(F32)
+        pair_copies[o, part.start // half].wait_recv()
+        mine[o, part, :] = (own + pair_in[o, part, :].astype(F32)).astype(BF16)
 
     def ring(slot, source, k):
         copy = pltpu.make_async_remote_copy(
@@ -222,36 +225,44 @@
         copy.start()
         return copy
 
-    top, bottom = slice(0, half), slice(half, toks)
     copies = [None] * 6
-    give(2)
-    give(1)
-    keep(2)
+    finish(top)
+    loads[4].wait()
+    give(2, top)
+    finish(bottom)
+    give(2, bottom)
+    keep(2, top)
     copies[0] = ring(0, mine.at[2, pl.ds(0, half)], 1)
+    give(1, bottom)
+    give(3, top)
+    keep(2, bottom)
     copies[1] = ring(1, mine.at[2, pl.ds(half, half)], ys - 1)
-    give(3)
-    keep(1)
+    keep(1, bottom)
     copies[2] = ring(2, mine.at[1, pl.ds(half, half)], 1)
-    give(0)
-    keep(3)
+    keep(3, top)
     copies[3] = ring(3, mine.at[3, pl.ds(0, half)], ys - 1)
-    keep(0)
+    give(1, top)
+    give(3, bottom)
+    keep(1, top)
+    keep(3, bottom)
     copies[0].wait_recv()
     ring_out[0] = (mine[1, top, :].astype(F32) + ring_in[0].astype(F32)).astype(BF16)
     copies[4] = ring(4, ring_out.at[0], 1)
     copies[1].wait_recv()
     ring_out[1] = (mine[3, bottom, :].astype(F32) + ring_in[1].astype(F32)).astype(BF16)
     copies[5] = ring(5, ring_out.at[1], ys - 1)
+    for part in (top, bottom):
+        give(0, part)
+    for part in (top, bottom):
+        keep(0, part)
     copies[2].wait_recv()
+    mine[0, bottom, :] = (mine[0, bottom, :].astype(F32) + ring_in[2].astype(F32)).astype(BF16)
     copies[3].wait_recv()
+    mine[0, top, :] = (mine[0, top, :].astype(F32) + ring_in[3].astype(F32)).astype(BF16)
     copies[4].wait_recv()
-    out_ref[top, :] = (
-        mine[0, top, :].astype(F32) + ring_in[3].astype(F32) + ring_in[4].astype(F32)
-    ).astype(BF16)
+    out_ref[top, :] = (mine[0, top, :].astype(F32) + ring_in[4].astype(F32)).astype(BF16)
     copies[5].wait_recv()
-    out_ref[bottom, :] = (
-        mine[0, bottom, :].astype(F32) + ring_in[2].astype(F32) + ring_in[5].astype(F32)
-    ).astype(BF16)
+    out_ref[bottom, :] = (mine[0, bottom, :].astype(F32) + ring_in[5].astype(F32)).astype(BF16)
 
     for copy in mom_copies + tot_copies + car_copies + list(pair_copies.values()) + copies:
         copy.wait_send()
@@ -298,7 +309,7 @@
             pltpu.VMEM((6, toks // 2, cols), BF16),
             dma((zs,)), dma((zs,)), dma((zs,)), dma((zs,)),
             dma((xs,)), dma((xs,)), dma((xs,)), dma((xs,)), dma((zs,)), dma((zs,)),
-            dma((ys,)), dma((ys,)), dma((6,)), dma((6,)), dma((5,)),
+            dma((2 * ys,)), dma((2 * ys,)), dma((6,)), dma((6,)), dma((5,)),
         ],
         compiler_params=pltpu.CompilerParams(
             collective_id=0, has_side_effects=True, vmem_limit_bytes=60 * 1024 * 1024

time: 59.9 us -> 59.1 us (0.987)
  Pallas kernels: 58 us -> 57.2 us
    pallas_call x1, Pallas kernels: 58 us -> 57.2 us  [on_device(): pl.pallas_call(functools.partial(kernel, xs, zs, ys), out_shape=jax.Shape...]
where the time goes in v3:
time: 59.1 us; the launch traced here: 59 us
  Pallas kernels  57.2 us (97%)
  local copies, waits for them, and re-layouts  1.78 us (3%)
    pallas_call x1, Pallas kernels, on_device(): pl.pallas_call(functools.partial(kernel, xs, zs, ys), out_shape=jax.Shape...  57.2 us
    unnamed x1, local copies, waits for them, and re-layouts  1.78 us

profile of v3, /device:TPU:1, one launch (start us, length us, event | category | flops | bytes accessed | tf_op | source)
XLA Modules:
  0.0 59.0 jit_solution(10391460000474929041)
XLA Ops:
  0.0 57.2 %shard_map.55 = bf16[512,384]{1,0:T(8,128)(2,1)} custom-call(bf16[512,512]{1,0:T(8,128)(2,1)} %q_hbm.1, bf16[512,512]{1,0:T(8,128)(2,1)} %k_hbm.1, bf16[512,512]{1,0:T(8,128)(2,1)} %v_hbm.1, f32[4,512]{1,0:T(4,128)} %g_hbm.1, bf16[512,3072]{1,0:T(8,128)(2,1)} %w_hbm.1), custom_call_target="tpu_custom_call" | custom-call | tf_op jit(solution)/shard_map/pallas_call | solution.py:279
  57.2 1.8 %copy.7 = bf16[512,384]{1,0:T(8,128)(2,1)} copy(bf16[512,384]{1,0:T(8,128)(2,1)} %shard_map.55) | data formatting | bytes 786432

commit v4 on v3

--- a/solution.py
+++ b/solution.py
@@ -88,24 +88,34 @@
 
     pl.semaphore_wait(barrier, len(peers))
 
-    mom_copies = []
+    pieces = [(n, pl.ds(n * (rows // 2), rows // 2)) for n in range(2)]
+
+    def z_copies(source, target, send, recv):
+        made = [[], []]
+        for n, piece in pieces:
+            for k in far_first(zs):
+                made[n].append(
+                    pltpu.make_async_remote_copy(
+                        src_ref=source.at[lax.rem(z + k, zs), piece], dst_ref=target.at[z, piece],
+                        send_sem=send.at[n * zs + k], recv_sem=recv.at[n * zs + k],
+                        device_id=z_peer(k), device_id_type=MESH,
+                    )
+                )
+        return made
+
+    dec_copies = []
     for k in far_first(zs):
-        mom_copies.append(
-            pltpu.make_async_remote_copy(
-                src_ref=mom_out.at[lax.rem(z + k, zs)], dst_ref=mom_in.at[z],
-                send_sem=s_mom.at[k], recv_sem=r_mom.at[k],
-                device_id=z_peer(k), device_id_type=MESH,
-            )
-        )
-        mom_copies[-1].start()
-        mom_copies.append(
+        dec_copies.append(
             pltpu.make_async_remote_copy(
                 src_ref=dec_out.at[lax.div(lax.rem(z + k, zs), per)], dst_ref=dec_in.at[z],
                 send_sem=s_dec.at[k], recv_sem=r_dec.at[k],
                 device_id=z_peer(k), device_id_type=MESH,
             )
         )
-        mom_copies[-1].start()
+        dec_copies[-1].start()
+    mom_copies = z_copies(mom_out, mom_in, s_mom, r_mom)
+    for copy in mom_copies[0] + mom_copies[1]:
+        copy.start()
     mom_in[z] = mom_out[z]
     dec_in[z] = dec_out[lax.div(z, per)]
     loads[3].wait()
@@ -123,63 +133,65 @@
     for h in range(heads // 2):
         within(h)
 
-    for copy in mom_copies:
+    for copy in dec_copies:
         copy.wait_recv()
-
-    state = jnp.zeros((rows, dim), F32)
     decay = jnp.ones((1, dim), F32)
     for j in range(zs):
-        pref[j] = state
         pref_decay[j] = decay
-        state = state * dec_in[j] + mom_in[j].astype(F32)
         decay = decay * dec_in[j]
-    tot_out[...] = state.astype(BF16)
     end_out[...] = decay
-    tot_copies = []
+    end_in[x] = decay
+    end_copies = []
     for k in far_first(xs):
-        tot_copies.append(
-            pltpu.make_async_remote_copy(
-                src_ref=tot_out, dst_ref=tot_in.at[x],
-                send_sem=s_tot.at[k], recv_sem=r_tot.at[k],
-                device_id=x_peer(k), device_id_type=MESH,
-            )
-        )
-        tot_copies[-1].start()
-        tot_copies.append(
+        end_copies.append(
             pltpu.make_async_remote_copy(
                 src_ref=end_out, dst_ref=end_in.at[x],
                 send_sem=s_end.at[k], recv_sem=r_end.at[k],
                 device_id=x_peer(k), device_id_type=MESH,
             )
         )
-        tot_copies[-1].start()
-    tot_in[x] = tot_out[...]
-    end_in[x] = end_out[...]
-    for copy in tot_copies:
+        end_copies[-1].start()
+
+    tot_copies = [[], []]
+    for n, piece in pieces:
+        for copy in mom_copies[n]:
+            copy.wait_recv()
+        state = jnp.zeros((rows // 2, dim), F32)
+        for j in range(zs):
+            pref[j, piece, :] = state
+            state = state * dec_in[j] + mom_in[j, piece, :].astype(F32)
+        tot_out[piece, :] = state.astype(BF16)
+        for k in far_first(xs):
+            tot_copies[n].append(
+                pltpu.make_async_remote_copy(
+                    src_ref=tot_out.at[piece], dst_ref=tot_in.at[x, piece],
+                    send_sem=s_tot.at[n * xs + k], recv_sem=r_tot.at[n * xs + k],
+                    device_id=x_peer(k), device_id_type=MESH,
+                )
+            )
+            tot_copies[n][-1].start()
+        tot_in[x, piece, :] = state.astype(BF16)
+
+    for copy in end_copies:
         copy.wait_recv()
-
-    before = jnp.zeros((rows, dim), F32)
-    for j in range(xs):
-        new = before * end_in[j] + tot_in[j].astype(F32)
-        before = jnp.where(j < x, new, before)
-    for j in range(zs):
-        car_out[j] = (pref[j] + pref_decay[j] * before).astype(BF16)
-    car_copies = []
-    for k in far_first(zs):
-        car_copies.append(
-            pltpu.make_async_remote_copy(
-                src_ref=car_out.at[lax.rem(z + k, zs)], dst_ref=car_in.at[z],
-                send_sem=s_car.at[k], recv_sem=r_car.at[k],
-                device_id=z_peer(k), device_id_type=MESH,
-            )
-        )
-        car_copies[-1].start()
+    car_copies = z_copies(car_out, car_in, s_car, r_car)
+    for n, piece in pieces:
+        for copy in tot_copies[n]:
+            copy.wait_recv()
+        before = jnp.zeros((rows // 2, dim), F32)
+        for j in range(xs):
+            new = before * end_in[j] + tot_in[j, piece, :].astype(F32)
+            before = jnp.where(j < x, new, before)
+        for j in range(zs):
+            car_out[j, piece, :] = (pref[j, piece, :] + pref_decay[j] * before).astype(BF16)
+        for copy in car_copies[n]:
+            copy.start()
     car_in[z] = car_out[z]
 
     for h in range(heads // 2, heads):
         within(h)
 
-    for copy in car_copies:
+    for copy in car_copies[0] + car_copies[1]:
         copy.wait_recv()
 
     top, bottom = slice(0, half), slice(half, toks)
@@ -264,7 +276,10 @@
     copies[5].wait_recv()
     out_ref[bottom, :] = (mine[0, bottom, :].astype(F32) + ring_in[5].astype(F32)).astype(BF16)
 
-    for copy in mom_copies + tot_copies + car_copies + list(pair_copies.values()) + copies:
+    sent = dec_copies + end_copies + list(pair_copies.values()) + copies
+    for pair in (mom_copies, tot_copies, car_copies):
+        sent += pair[0] + pair[1]
+    for copy in sent:
         copy.wait_send()
 
 
@@ -307,8 +322,8 @@
             pltpu.VMEM((ys, toks, cols), BF16),
             pltpu.VMEM((2, toks // 2, cols), BF16),
             pltpu.VMEM((6, toks // 2, cols), BF16),
-            dma((zs,)), dma((zs,)), dma((zs,)), dma((zs,)),
-            dma((xs,)), dma((xs,)), dma((xs,)), dma((xs,)), dma((zs,)), dma((zs,)),
+            dma((2 * zs,)), dma((2 * zs,)), dma((zs,)), dma((zs,)),
+            dma((2 * xs,)), dma((2 * xs,)), dma((xs,)), dma((xs,)), dma((2 * zs,)), dma((2 * zs,)),
             dma((2 * ys,)), dma((2 * ys,)), dma((6,)), dma((6,)), dma((5,)),
         ],
         compiler_params=pltpu.CompilerParams(

time: 59.1 us -> 60.9 us (1.030)
  Pallas kernels: 57.2 us -> 59 us
    pallas_call x1, Pallas kernels: 57.2 us -> 59 us  [on_device(): pl.pallas_call(functools.partial(kernel, xs, zs, ys), out_shape=jax.Shape...]
where the time goes in v4:
time: 60.9 us; the launch traced here: 60.8 us
  Pallas kernels  59 us (97%)
  local copies, waits for them, and re-layouts  1.78 us (3%)
    pallas_call x1, Pallas kernels, on_device(): pl.pallas_call(functools.partial(kernel, xs, zs, ys), out_shape=jax.Shape...  59 us
    unnamed x1, local copies, waits for them, and re-layouts  1.78 us

profile of v4, /device:TPU:1, one launch (start us, length us, event | category | flops | bytes accessed | tf_op | source)
XLA Modules:
  0.0 60.8 jit_solution(5399381702385483292)
XLA Ops:
  0.0 59.0 %shard_map.55 = bf16[512,384]{1,0:T(8,128)(2,1)} custom-call(bf16[512,512]{1,0:T(8,128)(2,1)} %q_hbm.1, bf16[512,512]{1,0:T(8,128)(2,1)} %k_hbm.1, bf16[512,512]{1,0:T(8,128)(2,1)} %v_hbm.1, f32[4,512]{1,0:T(4,128)} %g_hbm.1, bf16[512,3072]{1,0:T(8,128)(2,1)} %w_hbm.1), custom_call_target="tpu_custom_call" | custom-call | tf_op jit(solution)/shard_map/pallas_call | solution.py:294
  59.0 1.8 %copy.7 = bf16[512,384]{1,0:T(8,128)(2,1)} copy(bf16[512,384]{1,0:T(8,128)(2,1)} %shard_map.55) | data formatting | bytes 786432

commit v5 on v3

--- a/solution.py
+++ b/solution.py
@@ -98,6 +98,7 @@
             )
         )
         mom_copies[-1].start()
+    for k in far_first(zs):
         mom_copies.append(
             pltpu.make_async_remote_copy(
                 src_ref=dec_out.at[lax.div(lax.rem(z + k, zs), per)], dst_ref=dec_in.at[z],

time: 59.1 us -> 62.6 us (1.059)
  Pallas kernels: 57.2 us -> 60.6 us
    pallas_call x1, Pallas kernels: 57.2 us -> 60.6 us  [on_device(): pl.pallas_call(functools.partial(kernel, xs, zs, ys), out_shape=jax.Shape...]
where the time goes in v5:
time: 62.6 us; the launch traced here: 62.4 us
  Pallas kernels  60.6 us (97%)
  local copies, waits for them, and re-layouts  1.78 us (3%)
    pallas_call x1, Pallas kernels, on_device(): pl.pallas_call(functools.partial(kernel, xs, zs, ys), out_shape=jax.Shape...  60.6 us
    unnamed x1, local copies, waits for them, and re-layouts  1.78 us

profile of v5, /device:TPU:1, one launch (start us, length us, event | category | flops | bytes accessed | tf_op | source)
XLA Modules:
  0.0 62.4 jit_solution(2622316336173611713)
XLA Ops:
  0.0 60.6 %shard_map.55 = bf16[512,384]{1,0:T(8,128)(2,1)} custom-call(bf16[512,512]{1,0:T(8,128)(2,1)} %q_hbm.1, bf16[512,512]{1,0:T(8,128)(2,1)} %k_hbm.1, bf16[512,512]{1,0:T(8,128)(2,1)} %v_hbm.1, f32[4,512]{1,0:T(4,128)} %g_hbm.1, bf16[512,3072]{1,0:T(8,128)(2,1)} %w_hbm.1), custom_call_target="tpu_custom_call" | custom-call | tf_op jit(solution)/shard_map/pallas_call | solution.py:280
  60.6 1.8 %copy.7 = bf16[512,384]{1,0:T(8,128)(2,1)} copy(bf16[512,384]{1,0:T(8,128)(2,1)} %shard_map.55) | data formatting | bytes 786432
